TPU v7x, 512 devices: a whole 4x4x16 slice. The times are simulated.
512 devices in a mesh: blk: 16 (over z), pen: 32 (over x, y, core).
Axes of the slice: x: 4, y: 4, z: 16, core: 2. Of those that a mesh axis runs over, the one named last changes fastest.
Arguments:
- state: bfloat16 [16, 2, 32, 512, 512], P('blk', None, None, 'pen'), may hold values from -6 to 6
- inverse_x: bfloat16 [16, 2, 512, 512], P('blk')
- inverse_y: bfloat16 [16, 2, 512, 512], P('blk')
- rates: float32 [16, 3], P('blk'), may hold values from 0.05 to 0.4
- partner: int32 [16, 2], P('blk'), may hold values from 0 to 15
- face_side: int32 [16, 2], P('blk'), may hold values from 0 to 1
- orient: int32 [16, 2], P('blk'), may hold values from 0 to 1
- offset: int32 [16, 2], P('blk'), may hold values from 0 to 31
Outputs:
- relaxed: bfloat16 [16, 2, 32, 512, 512], P('blk', None, None, 'pen')
All inputs are finite; a program needn't handle non-finite values.
Results may differ from a plain program's by a relative error of at most 0.0058.
Values may be sent and summed in bfloat16 or wider, within the bound.
No kernel may reach another device: no remote copies, remote signals or barrier semaphores. Data moves between devices by JAX's collectives and lax.ppermute only.
A program may use at most 64 MiB of HBM per device.

v0:
```python
import jax
import jax.numpy as jnp
from jax import lax
from jax.sharding import PartitionSpec as P

STEPS = 2


def plane_ghosts(layers, partner_row, side_row, orient_row, offset_row, tile_rows):
    copies = jnp.broadcast_to(layers[None], (lax.axis_size("blk"),) + layers.shape)
    blocks = lax.all_to_all(copies, "blk", split_axis=0, concat_axis=0, tiled=True)
    lines = layers.shape[-1]
    rows_y = jnp.arange(lines, dtype=jnp.int32)
    result = []
    for which in range(2):
        piece = lax.dynamic_index_in_dim(blocks, partner_row[which], 0, keepdims=False)
        segment = lax.dynamic_index_in_dim(piece, side_row[which], 0, keepdims=False)
        mirrored = jnp.where(orient_row[which] == 1, lines - 1 - rows_y, rows_y)
        take_at = (mirrored + offset_row[which] * tile_rows) % lines
        result.append(jnp.take(segment, take_at, axis=-1))
    return result


def local(state, inverse_x, inverse_y, rates, partner, face_side, orient, offset):
    magnet = state[0]
    inv_x = inverse_x[0]
    inv_y = inverse_y[0]
    rate_row = rates[0]
    first_col = inv_x[:, :, 0].astype(jnp.float32)
    last_col = inv_x[:, :, -1].astype(jnp.float32)
    tile_rows = magnet.shape[2]
    planes = lax.all_to_all(magnet, "pen", split_axis=1, concat_axis=2, tiled=True)
    for repeat in range(STEPS):
        layers = jnp.stack([planes[..., 0], planes[..., -1]], axis=0)
        ghosts = plane_ghosts(layers, partner[0], face_side[0], orient[0], offset[0], tile_rows)
        interior = jnp.einsum("fax,fzyx->fzya", inv_x, planes, preferred_element_type=jnp.float32)
        edges = first_col[:, None, None, :] * ghosts[0].astype(jnp.float32)[..., None]
        edges = edges + last_col[:, None, None, :] * ghosts[1].astype(jnp.float32)[..., None]
        swept_x = (interior + edges).astype(jnp.bfloat16)
        swept_y = jnp.einsum("fcy,fzyx->fzcx", inv_y, swept_x, preferred_element_type=jnp.float32)
        proton = swept_y[0]
        carbon = swept_y[1]
        new_proton = proton - (rate_row[0] * proton + rate_row[2] * carbon)
        new_carbon = carbon - (rate_row[1] * carbon + rate_row[2] * proton)
        planes = jnp.stack([new_proton, new_carbon]).astype(jnp.bfloat16)
    magnet = lax.all_to_all(planes, "pen", split_axis=2, concat_axis=1, tiled=True)
    return magnet[None]


def solution(mesh):
    return jax.shard_map(
        local,
        mesh=mesh,
        in_specs=(
            P("blk", None, None, "pen", None),
            P("blk", None, None, None),
            P("blk", None, None, None),
            P("blk", None),
            P("blk", None),
            P("blk", None),
            P("blk", None),
            P("blk", None),
        ),
        out_specs=P("blk", None, None, "pen", None),
        check_vma=False,
    )
```

profile of v0, /device:TPU:1, one launch (start us, length us, event | category | flops | bytes accessed | tf_op | source)
XLA Modules:
  0.0 119.7 jit_solution(8040975433714026391)
XLA Ops:
  0.0 2.4 %copy.70 = bf16[1,2,32,16,512]{4,3,1,2,0:T(8,128)(2,1)} copy(bf16[1,2,32,16,512]{4,3,2,1,0:T(8,128)(2,1)} %param.10) | data formatting | bytes 2097152 | tf_op args[0]
  2.4 10.5 %all-to-all-start = ((bf16[2,32,16,512]{3,2,0,1:T(8,128)(2,1)}), bf16[2,32,16,512]{3,2,0,1:T(8,128)(2,1)S(1)}, u32[]{:S(2)}, u32[]{:S(2)}) async-start(bf16[2,32,16,512]{3,2,0,1:T(8,128)(2,1)} %bitcast.97), calls=%async_computation | async-start | bytes 2097152 | tf_op jit(solution)/shard_map/all_to_all | solution.py:32
  12.9 0.6 fusion.19
  16.0 0.7 fusion.18
  21.7 0.6 fusion.16
  23.4 0.7 fusion.17
  25.4 0.7 fusion.15
  26.1 3.8 %all-to-all-done = bf16[2,32,16,512]{3,2,0,1:T(8,128)(2,1)S(1)} async-done(((bf16[2,32,16,512]{3,2,0,1:T(8,128)(2,1)}), bf16[2,32,16,512]{3,2,0,1:T(8,128)(2,1)S(1)}, u32[]{:S(2)}, u32[]{:S(2)}) %all-to-all-start) | async-done | bytes 1048608 | tf_op jit(solution)/shard_map/all_to_all | solution.py:32
  30.0 0.3 slice_reduce_fusion.1
  30.3 0.7 broadcast_in_dim.20
  31.0 13.0 %all-to-all-start.1 = ((bf16[16,2,2,1,512]{4,2,3,1,0:T(2,128)(2,1)}), bf16[16,2,2,1,512]{4,2,3,1,0:T(2,128)(2,1)S(1)}, u32[]{:S(2)}, u32[]{:S(2)}) async-start(bf16[16,2,2,1,512]{4,2,3,1,0:T(2,128)(2,1)} %broadcast_in_dim.20), calls=%async_computation.1 | async-start | bytes 131072 | tf_op jit(solution)/shard_map/all_to_all | solution.py:11
  44.0 1.3 %convert_reduce_fusion.1 = (f32[2,512]{1,0:T(2,128)S(1)}, f32[2,512]{1,0:T(2,128)S(1)}) fusion(bf16[2,512,512]{2,1,0:T(8,128)(2,1)} %bitcast.102), kind=kLoop, calls=%fused_computation.20 | loop fusion | flops 2048 | bytes 12288 | tf_op jit(solution)/shard_map/convert_element_type | solution.py:29
  45.3 10.2 %all-to-all-done.1 = bf16[16,2,2,1,512]{4,2,3,1,0:T(2,128)(2,1)S(1)} async-done(((bf16[16,2,2,1,512]{4,2,3,1,0:T(2,128)(2,1)}), bf16[16,2,2,1,512]{4,2,3,1,0:T(2,128)(2,1)S(1)}, u32[]{:S(2)}, u32[]{:S(2)}) %all-to-all-start.1) | async-done | bytes 65568 | tf_op jit(solution)/shard_map/all_to_all | solution.py:11
  55.6 0.2 copy.49
  55.8 1.3 %gather_fusion = bf16[512,2]{1,0:T(8,128)(2,1)S(1)} fusion(bf16[2,512]{0,1:T(8,128)(2,1)S(1)} %bitcast.105, s32[1024]{0:T(1024)S(1)} %pad_clamp_fusion.1), kind=kCustom, calls=%fused_computation.clone | custom fusion | bytes 6144 | tf_op jit(solution)/shard_map/jit(_take)/gather | solution.py:20
  57.4 0.2 copy.51
  57.6 1.3 %gather_fusion.1 = bf16[512,2]{1,0:T(8,128)(2,1)S(1)} fusion(bf16[2,512]{0,1:T(8,128)(2,1)S(1)} %bitcast.106, s32[1024]{0:T(1024)S(1)} %pad_clamp_fusion), kind=kCustom, calls=%fused_computation.1.clone | custom fusion | bytes 6144 | tf_op jit(solution)/shard_map/jit(_take)/gather | solution.py:20
  58.9 0.1 bitcast_convert_fusion.2
  59.2 4.0 %convolution_bitcast_fusion.1 = f32[2,1,512,512]{2,3,0,1:T(8,128)} fusion(bf16[1,2,512,512]{3,2,1,0:T(8,128)(2,1)S(1)} %copy-done, bf16[2,512,512]{2,1,0:T(8,128)(2,1)S(1)} %bitcast.99, f32[2,512]{1,0:T(2,128)S(1)} %copy.52, f32[2,512]{1,0:T(2,128)S(1)} %get-tuple-element.7, f32[2,512]{1,0:T(2,128)S(1)} %copy.50, f32[2,512]{1,0:T(2,128)S(1)} %get-tuple-element.6, ...), kind=kOutput, calls=%fused_computation.7 | convolution fusion | flops 1076363264 | bytes 5259264 | tf_op jit(solution)/shard_map/fcy,fzyx->fzcx/dot_general | solution.py:40
  63.1 3.7 %subtract_convert_fusion.3 = (bf16[1,1,512,512]{2,3,0,1:T(8,128)(2,1)S(1)}, bf16[1,1,512,512]{2,3,0,1:T(8,128)(2,1)S(1)}) fusion(f32[2,1,512,512]{2,3,0,1:T(8,128)} %convolution_bitcast_fusion.1, f32[]{:T(128)} %bitcast.27, f32[]{:T(128)} %bitcast.26, f32[]{:T(128)} %bitcast.30), kind=kLoop, calls=%fused_computation.18 | loop fusion | flops 2621440 | bytes 3145740 | tf_op jit(solution)/shard_map/convert.13
  67.0 15.5 %all_to_all.31 = bf16[16,2,2,1,512]{4,2,3,1,0:T(2,128)(2,1)S(1)} all-to-all(bf16[16,2,2,1,512]{4,2,3,1,0:T(2,128)(2,1)S(1)} %broadcast_in_dim.22), channel_id=1, replica_groups=mesh['blk'=16,'pen'=32] {'blk'}, dimensions={0} | all-to-all | bytes 131072 | tf_op jit(solution)/shard_map/all_to_all | solution.py:11
  82.5 0.2 copy.55
  82.7 1.3 %gather_fusion.2 = bf16[512,2]{1,0:T(8,128)(2,1)S(1)} fusion(bf16[2,512]{0,1:T(8,128)(2,1)S(1)} %bitcast.103, s32[1024]{0:T(1024)S(1)} %pad_clamp_fusion.1), kind=kCustom, calls=%fused_computation.2.clone | custom fusion | bytes 6144 | tf_op jit(solution)/shard_map/jit(_take)/gather | solution.py:20
  84.0 0.8 bitcast_convert_fusion.1
  84.9 0.2 copy.57
  85.1 1.3 %gather_fusion.3 = bf16[512,2]{1,0:T(8,128)(2,1)S(1)} fusion(bf16[2,512]{0,1:T(8,128)(2,1)S(1)} %bitcast.104, s32[1024]{0:T(1024)S(1)} %pad_clamp_fusion), kind=kCustom, calls=%fused_computation.3.clone | custom fusion | bytes 6144 | tf_op jit(solution)/shard_map/jit(_take)/gather | solution.py:20
  86.5 0.7 bitcast_convert_fusion
  87.3 3.9 %convolution_bitcast_fusion = f32[2,1,512,512]{2,3,0,1:T(8,128)} fusion(bf16[1,2,512,512]{3,2,1,0:T(8,128)(2,1)S(1)} %copy-done, bf16[1,512,512]{1,2,0:T(8,128)(2,1)S(1)} %bitcast.101, bf16[1,512,512]{1,2,0:T(8,128)(2,1)S(1)} %bitcast.100, f32[2,512]{1,0:T(2,128)S(1)} %copy.58, f32[2,512]{1,0:T(2,128)S(1)} %copy.56, f32[2,512]{1,0:T(2,128)} %copy-done.3, ...), kind=kOutput, calls=%fused_computation.6 | convolution fusion | flops 1076887552 | bytes 5259264 | tf_op jit(solution)/shard_map/fcy,fzyx->fzcx/dot_general | solution.py:40
  91.2 3.7 %subtract_convert_fusion.1 = (bf16[1,1,512,512]{2,3,0,1:T(8,128)(2,1)S(1)}, bf16[1,1,512,512]{2,3,0,1:T(8,128)(2,1)S(1)}) fusion(f32[2,1,512,512]{2,3,0,1:T(8,128)} %convolution_bitcast_fusion, f32[]{:T(128)} %bitcast.27, f32[]{:T(128)} %bitcast.26, f32[]{:T(128)} %bitcast.30), kind=kLoop, calls=%fused_computation.16 | loop fusion | flops 2621440 | bytes 3145740 | tf_op jit(solution)/shard_map/convert.6
  95.1 1.0 copy.60
  96.1 22.5 %all_to_all.32 = bf16[2,1,512,512]{3,0,1,2:T(2,128)(2,1)S(1)} all-to-all(bf16[2,1,512,512]{3,0,1,2:T(2,128)(2,1)S(1)} %copy.60), channel_id=1, replica_groups=mesh['blk'=16,'pen'=32] {'pen'}, dimensions={2} | all-to-all | bytes 2097152 | tf_op jit(solution)/shard_map/all_to_all | solution.py:46
  118.5 1.1 copy.61
  (40 shorter events, 1.0 us)
Async XLA Ops:
  0.0 59.2 %copy-start = (bf16[1,2,512,512]{3,2,1,0:T(8,128)(2,1)S(1)}, bf16[1,2,512,512]{3,2,1,0:T(8,128)(2,1)}, u32[]{:S(2)}) copy-start(bf16[1,2,512,512]{3,2,1,0:T(8,128)(2,1)} %param.12) | copy-start | bytes 3145732
  0.0 12.9 %copy-start.6 = (s32[1,2]{1,0:T(1,128)S(1)}, s32[1,2]{1,0:T(1,128)}, u32[]{:S(2)}) copy-start(s32[1,2]{1,0:T(1,128)} %param.14) | copy-start | bytes 28
  0.0 16.0 %copy-start.7 = (s32[1,2]{1,0:T(1,128)S(1)}, s32[1,2]{1,0:T(1,128)}, u32[]{:S(2)}) copy-start(s32[1,2]{1,0:T(1,128)} %param.15) | copy-start | bytes 28
  0.0 21.6 %copy-start.8 = (s32[1,2]{1,0:T(1,128)S(1)}, s32[1,2]{1,0:T(1,128)}, u32[]{:S(2)}) copy-start(s32[1,2]{1,0:T(1,128)} %param.16) | copy-start | bytes 28
  0.0 23.4 %copy-start.9 = (s32[1,2]{1,0:T(1,128)S(1)}, s32[1,2]{1,0:T(1,128)}, u32[]{:S(2)}) copy-start(s32[1,2]{1,0:T(1,128)} %param.17) | copy-start | bytes 28
  0.0 25.4 %copy-start.2 = (f32[1,3]{1,0:T(1,128)S(1)}, f32[1,3]{1,0:T(1,128)}, u32[]{:S(2)}) copy-start(f32[1,3]{1,0:T(1,128)} %param.13) | copy-start | bytes 40
  2.4 27.5 %all-to-all-start = ((bf16[2,32,16,512]{3,2,0,1:T(8,128)(2,1)}), bf16[2,32,16,512]{3,2,0,1:T(8,128)(2,1)S(1)}, u32[]{:S(2)}, u32[]{:S(2)}) async-start(bf16[2,32,16,512]{3,2,0,1:T(8,128)(2,1)} %bitcast.97), calls=%async_computation | async-start | bytes 2097152 | tf_op jit(solution)/shard_map/all_to_all | solution.py:32
  25.3 32.0 %copy-start.4 = (pred[512]{0:T(512)(128)(4,1)}, pred[512]{0:T(512)(128)(4,1)S(1)}, u32[]{:S(2)}) copy-start(pred[512]{0:T(512)(128)(4,1)S(1)} %compare_and_fusion.1) | copy-start | bytes 1540
  31.0 24.6 %all-to-all-start.1 = ((bf16[16,2,2,1,512]{4,2,3,1,0:T(2,128)(2,1)}), bf16[16,2,2,1,512]{4,2,3,1,0:T(2,128)(2,1)S(1)}, u32[]{:S(2)}, u32[]{:S(2)}) async-start(bf16[16,2,2,1,512]{4,2,3,1,0:T(2,128)(2,1)} %broadcast_in_dim.20), calls=%async_computation.1 | async-start | bytes 131072 | tf_op jit(solution)/shard_map/all_to_all | solution.py:11
  44.0 19.2 %copy-start.5 = (pred[512]{0:T(512)(128)(4,1)}, pred[512]{0:T(512)(128)(4,1)S(1)}, u32[]{:S(2)}) copy-start(pred[512]{0:T(512)(128)(4,1)S(1)} %compare_and_fusion) | copy-start | bytes 1540
  45.3 17.8 %copy-start.3 = (f32[2,512]{1,0:T(2,128)}, f32[2,512]{1,0:T(2,128)S(1)}, u32[]{:S(2)}) copy-start(f32[2,512]{1,0:T(2,128)S(1)} %get-tuple-element.7) | copy-start | bytes 12292
  66.9 20.4 %copy-start.1 = (bf16[1,2,512,512]{3,2,1,0:T(8,128)(2,1)S(1)}, bf16[1,2,512,512]{3,2,1,0:T(8,128)(2,1)}, u32[]{:S(2)}) copy-start(bf16[1,2,512,512]{3,2,1,0:T(8,128)(2,1)} %param.11) | copy-start | bytes 3145732
where the time goes:
time: 120 us
  blocking collectives  37.9 us (32%)
  starting transfers between devices  23.4 us (20%)
  local copies, waits for them, and re-layouts  15.3 us (13%)
  waiting for transfers between devices  14 us (12%)
  other arithmetic  10.9 us (9%)
  between operations  10.2 us (8%)
  matrix products  7.86 us (7%)
    all_to_all x1, blocking collectives, local(): lax.all_to_all(planes, 'pen', split_axis=2, concat_axis=1, tiled=True)  22.5 us
    all_to_all x1, blocking collectives, plane_ghosts(): lax.all_to_all(copies, 'blk', split_axis=0, concat_axis=0, tiled=True)  15.5 us
    all_to_all x1, starting transfers between devices, plane_ghosts(): lax.all_to_all(copies, 'blk', split_axis=0, concat_axis=0, tiled=True)  13 us
    all_to_all x1, starting transfers between devices, local(): lax.all_to_all(magnet, 'pen', split_axis=1, concat_axis=2, tiled=True)  10.5 us
    all_to_all x1, waiting for transfers between devices, plane_ghosts(): lax.all_to_all(copies, 'blk', split_axis=0, concat_axis=0, tiled=True)  10.2 us
    dot_general x2, matrix products, local(): jnp.einsum('fcy,fzyx->fzcx', inv_y, swept_x, preferred_element_type=jnp.f...  7.86 us
    another operation x2, other arithmetic  7.49 us
    gather x4, local copies, waits for them, and re-layouts, plane_ghosts(): result.append(jnp.take(segment, take_at, axis=-1))  5.36 us
  transfers between devices with their start and end apart: 2, of which 2 were waited for; matrix products, arithmetic and copies ran while one was open for 4% of the time, Pallas kernels for 0%

commit v1 on v0

--- a/solution.py
+++ b/solution.py
@@ -6,9 +6,25 @@
 STEPS = 2
 
 
+def exchange_in_pairs(x, axis, split, join):
+    ways, here = (lax.axis_size(axis), lax.axis_index(axis))
+    width = x.shape[split] // ways
+    shape = list(x.shape)
+    shape[split] = width
+    height = shape[join]
+    shape[join] = height * ways
+    full = jnp.zeros(shape, x.dtype)
+    for mask in range(ways):
+        part = lax.dynamic_slice_in_dim(x, (here ^ mask) * width, width, axis=split)
+        if mask:
+            part = lax.ppermute(part, axis, [(d, d ^ mask) for d in range(ways)])
+        full = lax.dynamic_update_slice_in_dim(full, part, (here ^ mask) * height, axis=join)
+    return full
+
+
 def plane_ghosts(layers, partner_row, side_row, orient_row, offset_row, tile_rows):
     copies = jnp.broadcast_to(layers[None], (lax.axis_size("blk"),) + layers.shape)
-    blocks = lax.all_to_all(copies, "blk", split_axis=0, concat_axis=0, tiled=True)
+    blocks = exchange_in_pairs(copies, "blk", 0, 0)
     lines = layers.shape[-1]
     rows_y = jnp.arange(lines, dtype=jnp.int32)
     result = []

time: 120 us -> 274 us (2.28)
  starting transfers between devices: 23.4 us -> 159 us
  local copies, waits for them, and re-layouts: 15.3 us -> 52.2 us
  waiting for transfers between devices: 14 us -> 3.49 us
  blocking collectives: 37.9 us -> 28.6 us
    ppermute x0 -> x30, starting transfers between devices: none -> 149 us  [exchange_in_pairs(): part = lax.ppermute(part, axis, [(d, d ^ mask) for d in range(ways)])]
    dynamic_update_slice x0 -> x32, local copies, waits for them, and re-layouts: none -> 23.3 us  [exchange_in_pairs(): lax.dynamic_update_slice_in_dim(full, part, (here ^ mask) * height, axis=...]
    all_to_all x1 -> x0, blocking collectives: 15.5 us -> none  [plane_ghosts(): lax.all_to_all(copies, 'blk', split_axis=0, concat_axis=0, tiled=True)]
    all_to_all x1 -> x0, starting transfers between devices: 13 us -> none  [plane_ghosts(): lax.all_to_all(copies, 'blk', split_axis=0, concat_axis=0, tiled=True)]
    all_to_all x1 -> x0, waiting for transfers between devices: 10.2 us -> none  [plane_ghosts(): lax.all_to_all(copies, 'blk', split_axis=0, concat_axis=0, tiled=True)]
    another operation x0 -> x4, local copies, waits for them, and re-layouts: none -> 7.82 us
    ppermute x0 -> x30, local copies, waits for them, and re-layouts: none -> 6.26 us  [exchange_in_pairs(): part = lax.ppermute(part, axis, [(d, d ^ mask) for d in range(ways)])]
    all_to_all x1, blocking collectives: 22.5 us -> 28.6 us  [local(): lax.all_to_all(planes, 'pen', split_axis=2, concat_axis=1, tiled=True)]
  transfers between devices with their start and end apart: 2 -> 31, of which waited for: 2 -> 1; matrix products, arithmetic and copies ran while one was open for 4% -> 14% of each run, Pallas kernels for 0% -> 0%
where the time goes in v1:
time: 274 us; the launch traced here: 271 us
  starting transfers between devices  159 us (58%)
  local copies, waits for them, and re-layouts  52.2 us (19%)
  blocking collectives  28.6 us (10%)
  between operations  10.7 us (4%)
  other arithmetic  9.6 us (4%)
  matrix products  7.79 us (3%)
  waiting for transfers between devices  3.49 us (1%)
    ppermute x30, starting transfers between devices, exchange_in_pairs(): part = lax.ppermute(part, axis, [(d, d ^ mask) for d in range(ways)])  149 us
    all_to_all x1, blocking collectives, local(): lax.all_to_all(planes, 'pen', split_axis=2, concat_axis=1, tiled=True)  28.6 us
    dynamic_update_slice x32, local copies, waits for them, and re-layouts, exchange_in_pairs(): lax.dynamic_update_slice_in_dim(full, part, (here ^ mask) * height, axis=...  23.3 us
    all_to_all x1, starting transfers between devices, local(): lax.all_to_all(magnet, 'pen', split_axis=1, concat_axis=2, tiled=True)  10.5 us
    dot_general x2, matrix products, local(): jnp.einsum('fcy,fzyx->fzcx', inv_y, swept_x, preferred_element_type=jnp.f...  7.79 us
    another operation x2, other arithmetic  7.65 us
    ppermute x30, local copies, waits for them, and re-layouts, exchange_in_pairs(): part = lax.ppermute(part, axis, [(d, d ^ mask) for d in range(ways)])  6.26 us
    gather x4, local copies, waits for them, and re-layouts, plane_ghosts(): result.append(jnp.take(segment, take_at, axis=-1))  5.95 us
  transfers between devices with their start and end apart: 31, of which 1 were waited for; matrix products, arithmetic and copies ran while one was open for 14% of the time, Pallas kernels for 0%

profile of v1, /device:TPU:1, one launch (start us, length us, event | category | flops | bytes accessed | tf_op | source)
XLA Modules:
  0.0 271.4 jit_solution(13799913106358223308)
XLA Ops:
  2.5 10.5 %all-to-all-start = ((bf16[2,32,16,512]{3,2,0,1:T(8,128)(2,1)}), bf16[2,32,16,512]{3,2,0,1:T(8,128)(2,1)S(1)}, u32[]{:S(2)}, u32[]{:S(2)}) async-start(bf16[2,32,16,512]{3,2,0,1:T(8,128)(2,1)} %bitcast.101), calls=%async_computation | async-start | bytes 2097152 | tf_op jit(solution)/shard_map/all_to_all | solution.py:48
  26.5 3.4 %all-to-all-done = bf16[2,32,16,512]{3,2,0,1:T(8,128)(2,1)S(1)} async-done(((bf16[2,32,16,512]{3,2,0,1:T(8,128)(2,1)}), bf16[2,32,16,512]{3,2,0,1:T(8,128)(2,1)S(1)}, u32[]{:S(2)}, u32[]{:S(2)}) %all-to-all-start) | async-done | bytes 1048608 | tf_op jit(solution)/shard_map/all_to_all | solution.py:48
  32.5 4.6 %collective-permute-start.1 = (bf16[1,2,2,1,512]{4,2,1,3,0:T(2,128)(2,1)S(1)}, bf16[1,2,2,1,512]{4,2,1,3,0:T(2,128)(2,1)S(1)}, u32[]{:S(2)}, u32[]{:S(2)}) collective-permute-start(bf16[1,2,2,1,512]{4,2,1,3,0:T(2,128)(2,1)S(1)} %maximum_bitcast_fusion), channel_id=1, source_target_pairs={{0,64},{32,96},{64,0},{96,32},{128,192},{160,224},{192,128},{224,1... | collective-permute-start | bytes 12296 | tf_op jit(solution)/shard_map/ppermute | solution.py:20
  37.1 2.8 %collective-permute-start.2 = (bf16[1,2,2,1,512]{4,2,1,3,0:T(2,128)(2,1)S(1)}, bf16[1,2,2,1,512]{4,2,1,3,0:T(2,128)(2,1)S(1)}, u32[]{:S(2)}, u32[]{:S(2)}) collective-permute-start(bf16[1,2,2,1,512]{4,2,1,3,0:T(2,128)(2,1)S(1)} %maximum_bitcast_fusion), channel_id=1, source_target_pairs={{0,96},{32,64},{64,32},{96,0},{128,224},{160,192},{192,160},{224,1... | collective-permute-start | bytes 12296 | tf_op jit(solution)/shard_map/ppermute | solution.py:20
  39.9 8.0 %collective-permute-start.3 = (bf16[1,2,2,1,512]{4,2,1,3,0:T(2,128)(2,1)S(1)}, bf16[1,2,2,1,512]{4,2,1,3,0:T(2,128)(2,1)S(1)}, u32[]{:S(2)}, u32[]{:S(2)}) collective-permute-start(bf16[1,2,2,1,512]{4,2,1,3,0:T(2,128)(2,1)S(1)} %maximum_bitcast_fusion), channel_id=1, source_target_pairs={{0,128},{32,160},{64,192},{96,224},{128,0},{160,32},{192,64},{224,... | collective-permute-start | bytes 12296 | tf_op jit(solution)/shard_map/ppermute | solution.py:20
  49.8 2.9 %broadcast.115.clone = bf16[16,2,2,1,512]{2,4,3,1,0:T(8,128)(2,1)} broadcast(bf16[]{:T(256)} %constant.176.clone.1), dimensions={} | broadcast | bytes 65538 | tf_op jit(solution)/shard_map/broadcast.5
  53.4 9.3 %collective-permute-start.5 = (bf16[1,2,2,1,512]{4,2,1,3,0:T(2,128)(2,1)S(1)}, bf16[1,2,2,1,512]{4,2,1,3,0:T(2,128)(2,1)S(1)}, u32[]{:S(2)}, u32[]{:S(2)}) collective-permute-start(bf16[1,2,2,1,512]{4,2,1,3,0:T(2,128)(2,1)S(1)} %maximum_bitcast_fusion), channel_id=1, source_target_pairs={{0,192},{32,224},{64,128},{96,160},{128,64},{160,96},{192,0},{224,... | collective-permute-start | bytes 12296 | tf_op jit(solution)/shard_map/ppermute | solution.py:20
  66.5 12.6 %collective-permute-start.7 = (bf16[1,2,2,1,512]{4,2,1,3,0:T(2,128)(2,1)S(1)}, bf16[1,2,2,1,512]{4,2,1,3,0:T(2,128)(2,1)S(1)}, u32[]{:S(2)}, u32[]{:S(2)}) collective-permute-start(bf16[1,2,2,1,512]{4,2,1,3,0:T(2,128)(2,1)S(1)} %maximum_bitcast_fusion), channel_id=1, source_target_pairs={{0,256},{32,288},{64,320},{96,352},{128,384},{160,416},{192,448},{... | collective-permute-start | bytes 12296 | tf_op jit(solution)/shard_map/ppermute | solution.py:20
  82.9 7.1 %collective-permute-start.9 = (bf16[1,2,2,1,512]{4,2,1,3,0:T(2,128)(2,1)S(1)}, bf16[1,2,2,1,512]{4,2,1,3,0:T(2,128)(2,1)S(1)}, u32[]{:S(2)}, u32[]{:S(2)}) collective-permute-start(bf16[1,2,2,1,512]{4,2,1,3,0:T(2,128)(2,1)S(1)} %maximum_bitcast_fusion), channel_id=1, source_target_pairs={{0,320},{32,352},{64,256},{96,288},{128,448},{160,480},{192,384},{... | collective-permute-start | bytes 12296 | tf_op jit(solution)/shard_map/ppermute | solution.py:20
  91.0 4.2 %collective-permute-start.10 = (bf16[1,2,2,1,512]{4,2,1,3,0:T(2,128)(2,1)S(1)}, bf16[1,2,2,1,512]{4,2,1,3,0:T(2,128)(2,1)S(1)}, u32[]{:S(2)}, u32[]{:S(2)}) collective-permute-start(bf16[1,2,2,1,512]{4,2,1,3,0:T(2,128)(2,1)S(1)} %maximum_bitcast_fusion), channel_id=1, source_target_pairs={{0,352},{32,320},{64,288},{96,256},{128,480},{160,448},{192,416},{... | collective-permute-start | bytes 12296 | tf_op jit(solution)/shard_map/ppermute | solution.py:20
  96.1 5.4 %collective-permute-start.11 = (bf16[1,2,2,1,512]{4,2,1,3,0:T(2,128)(2,1)S(1)}, bf16[1,2,2,1,512]{4,2,1,3,0:T(2,128)(2,1)S(1)}, u32[]{:S(2)}, u32[]{:S(2)}) collective-permute-start(bf16[1,2,2,1,512]{4,2,1,3,0:T(2,128)(2,1)S(1)} %maximum_bitcast_fusion), channel_id=1, source_target_pairs={{0,384},{32,416},{64,448},{96,480},{128,256},{160,288},{192,320},{... | collective-permute-start | bytes 12296 | tf_op jit(solution)/shard_map/ppermute | solution.py:20
  102.5 4.6 %collective-permute-start.12 = (bf16[1,2,2,1,512]{4,2,1,3,0:T(2,128)(2,1)S(1)}, bf16[1,2,2,1,512]{4,2,1,3,0:T(2,128)(2,1)S(1)}, u32[]{:S(2)}, u32[]{:S(2)}) collective-permute-start(bf16[1,2,2,1,512]{4,2,1,3,0:T(2,128)(2,1)S(1)} %maximum_bitcast_fusion), channel_id=1, source_target_pairs={{0,416},{32,384},{64,480},{96,448},{128,288},{160,256},{192,352},{... | collective-permute-start | bytes 12296 | tf_op jit(solution)/shard_map/ppermute | solution.py:20
  108.0 7.7 %collective-permute-start.13 = (bf16[1,2,2,1,512]{4,2,1,3,0:T(2,128)(2,1)S(1)}, bf16[1,2,2,1,512]{4,2,1,3,0:T(2,128)(2,1)S(1)}, u32[]{:S(2)}, u32[]{:S(2)}) collective-permute-start(bf16[1,2,2,1,512]{4,2,1,3,0:T(2,128)(2,1)S(1)} %maximum_bitcast_fusion), channel_id=1, source_target_pairs={{0,448},{32,480},{64,384},{96,416},{128,320},{160,352},{192,256},{... | collective-permute-start | bytes 12296 | tf_op jit(solution)/shard_map/ppermute | solution.py:20
  128.5 3.9 %convolution_bitcast_fusion.1 = f32[2,1,512,512]{2,3,0,1:T(8,128)} fusion(bf16[1,2,512,512]{3,2,1,0:T(8,128)(2,1)S(1)} %copy-done, bf16[2,512,512]{2,1,0:T(8,128)(2,1)S(1)} %bitcast.105, f32[2,512]{1,0:T(2,128)S(1)} %copy.165, f32[2,512]{1,0:T(2,128)S(1)} %get-tuple-element.7, f32[2,512]{1,0:T(2,128)S(1)} %copy.164, f32[2,512]{1,0:T(2,128)S(1)} %get-tuple-element.6, ...), kind=kOutput, calls=%fused_computation.7 | convolution fusion | flops 1076363264 | bytes 5259264 | tf_op jit(solution)/shard_map/fcy,fzyx->fzcx/dot_general | solution.py:56
  132.5 3.8 %subtract_convert_fusion.3 = (bf16[1,1,512,512]{2,3,0,1:T(8,128)(2,1)S(1)}, bf16[1,1,512,512]{2,3,0,1:T(8,128)(2,1)S(1)}) fusion(f32[2,1,512,512]{2,3,0,1:T(8,128)} %convolution_bitcast_fusion.1, f32[]{:T(128)} %bitcast.27, f32[]{:T(128)} %bitcast.26, f32[]{:T(128)} %bitcast.30), kind=kLoop, calls=%fused_computation.18 | loop fusion | flops 2621440 | bytes 3145740 | tf_op jit(solution)/shard_map/convert.13
  136.6 3.1 %collective-permute-start.15 = (bf16[1,2,2,1,512]{4,2,1,3,0:T(2,128)(2,1)S(1)}, bf16[1,2,2,1,512]{4,2,1,3,0:T(2,128)(2,1)S(1)}, u32[]{:S(2)}, u32[]{:S(2)}) collective-permute-start(bf16[1,2,2,1,512]{4,2,1,3,0:T(2,128)(2,1)S(1)} %maximum_bitcast_fusion.1), channel_id=1, source_target_pairs={{0,32},{32,0},{64,96},{96,64},{128,160},{160,128},{192,224},{224,1... | collective-permute-start | bytes 12296 | tf_op jit(solution)/shard_map/ppermute | solution.py:20
  139.6 5.4 %collective-permute-start.16 = (bf16[1,2,2,1,512]{4,2,1,3,0:T(2,128)(2,1)S(1)}, bf16[1,2,2,1,512]{4,2,1,3,0:T(2,128)(2,1)S(1)}, u32[]{:S(2)}, u32[]{:S(2)}) collective-permute-start(bf16[1,2,2,1,512]{4,2,1,3,0:T(2,128)(2,1)S(1)} %maximum_bitcast_fusion.1), channel_id=1, source_target_pairs={{0,64},{32,96},{64,0},{96,32},{128,192},{160,224},{192,128},{224,1... | collective-permute-start | bytes 12296 | tf_op jit(solution)/shard_map/ppermute | solution.py:20
  147.0 6.8 %collective-permute-start.18 = (bf16[1,2,2,1,512]{4,2,1,3,0:T(2,128)(2,1)S(1)}, bf16[1,2,2,1,512]{4,2,1,3,0:T(2,128)(2,1)S(1)}, u32[]{:S(2)}, u32[]{:S(2)}) collective-permute-start(bf16[1,2,2,1,512]{4,2,1,3,0:T(2,128)(2,1)S(1)} %maximum_bitcast_fusion.1), channel_id=1, source_target_pairs={{0,128},{32,160},{64,192},{96,224},{128,0},{160,32},{192,64},{224,... | collective-permute-start | bytes 12296 | tf_op jit(solution)/shard_map/ppermute | solution.py:20
  156.2 2.9 %broadcast.115 = bf16[16,2,2,1,512]{2,4,3,1,0:T(8,128)(2,1)} broadcast(bf16[]{:T(256)} %constant.176.clone.1), dimensions={} | broadcast | bytes 65538 | tf_op jit(solution)/shard_map/broadcast.5
  159.8 5.6 %collective-permute-start.20 = (bf16[1,2,2,1,512]{4,2,1,3,0:T(2,128)(2,1)S(1)}, bf16[1,2,2,1,512]{4,2,1,3,0:T(2,128)(2,1)S(1)}, u32[]{:S(2)}, u32[]{:S(2)}) collective-permute-start(bf16[1,2,2,1,512]{4,2,1,3,0:T(2,128)(2,1)S(1)} %maximum_bitcast_fusion.1), channel_id=1, source_target_pairs={{0,192},{32,224},{64,128},{96,160},{128,64},{160,96},{192,0},{224,... | collective-permute-start | bytes 12296 | tf_op jit(solution)/shard_map/ppermute | solution.py:20
  166.4 5.4 %collective-permute-start.21 = (bf16[1,2,2,1,512]{4,2,1,3,0:T(2,128)(2,1)S(1)}, bf16[1,2,2,1,512]{4,2,1,3,0:T(2,128)(2,1)S(1)}, u32[]{:S(2)}, u32[]{:S(2)}) collective-permute-start(bf16[1,2,2,1,512]{4,2,1,3,0:T(2,128)(2,1)S(1)} %maximum_bitcast_fusion.1), channel_id=1, source_target_pairs={{0,224},{32,192},{64,160},{96,128},{128,96},{160,64},{192,32},{224... | collective-permute-start | bytes 12296 | tf_op jit(solution)/shard_map/ppermute | solution.py:20
  172.7 7.8 %collective-permute-start.22 = (bf16[1,2,2,1,512]{4,2,1,3,0:T(2,128)(2,1)S(1)}, bf16[1,2,2,1,512]{4,2,1,3,0:T(2,128)(2,1)S(1)}, u32[]{:S(2)}, u32[]{:S(2)}) collective-permute-start(bf16[1,2,2,1,512]{4,2,1,3,0:T(2,128)(2,1)S(1)} %maximum_bitcast_fusion.1), channel_id=1, source_target_pairs={{0,256},{32,288},{64,320},{96,352},{128,384},{160,416},{192,448},{... | collective-permute-start | bytes 12296 | tf_op jit(solution)/shard_map/ppermute | solution.py:20
  181.4 5.3 %collective-permute-start.23 = (bf16[1,2,2,1,512]{4,2,1,3,0:T(2,128)(2,1)S(1)}, bf16[1,2,2,1,512]{4,2,1,3,0:T(2,128)(2,1)S(1)}, u32[]{:S(2)}, u32[]{:S(2)}) collective-permute-start(bf16[1,2,2,1,512]{4,2,1,3,0:T(2,128)(2,1)S(1)} %maximum_bitcast_fusion.1), channel_id=1, source_target_pairs={{0,288},{32,256},{64,352},{96,320},{128,416},{160,384},{192,480},{... | collective-permute-start | bytes 12296 | tf_op jit(solution)/shard_map/ppermute | solution.py:20
  187.7 5.4 %collective-permute-start.24 = (bf16[1,2,2,1,512]{4,2,1,3,0:T(2,128)(2,1)S(1)}, bf16[1,2,2,1,512]{4,2,1,3,0:T(2,128)(2,1)S(1)}, u32[]{:S(2)}, u32[]{:S(2)}) collective-permute-start(bf16[1,2,2,1,512]{4,2,1,3,0:T(2,128)(2,1)S(1)} %maximum_bitcast_fusion.1), channel_id=1, source_target_pairs={{0,320},{32,352},{64,256},{96,288},{128,448},{160,480},{192,384},{... | collective-permute-start | bytes 12296 | tf_op jit(solution)/shard_map/ppermute | solution.py:20
  194.0 6.8 %collective-permute-start.25 = (bf16[1,2,2,1,512]{4,2,1,3,0:T(2,128)(2,1)S(1)}, bf16[1,2,2,1,512]{4,2,1,3,0:T(2,128)(2,1)S(1)}, u32[]{:S(2)}, u32[]{:S(2)}) collective-permute-start(bf16[1,2,2,1,512]{4,2,1,3,0:T(2,128)(2,1)S(1)} %maximum_bitcast_fusion.1), channel_id=1, source_target_pairs={{0,352},{32,320},{64,288},{96,256},{128,480},{160,448},{192,416},{... | collective-permute-start | bytes 12296 | tf_op jit(solution)/shard_map/ppermute | solution.py:20
  201.8 2.9 %collective-permute-start.26 = (bf16[1,2,2,1,512]{4,2,1,3,0:T(2,128)(2,1)S(1)}, bf16[1,2,2,1,512]{4,2,1,3,0:T(2,128)(2,1)S(1)}, u32[]{:S(2)}, u32[]{:S(2)}) collective-permute-start(bf16[1,2,2,1,512]{4,2,1,3,0:T(2,128)(2,1)S(1)} %maximum_bitcast_fusion.1), channel_id=1, source_target_pairs={{0,384},{32,416},{64,448},{96,480},{128,256},{160,288},{192,320},{... | collective-permute-start | bytes 12296 | tf_op jit(solution)/shard_map/ppermute | solution.py:20
  205.6 6.4 %collective-permute-start.27 = (bf16[1,2,2,1,512]{4,2,1,3,0:T(2,128)(2,1)S(1)}, bf16[1,2,2,1,512]{4,2,1,3,0:T(2,128)(2,1)S(1)}, u32[]{:S(2)}, u32[]{:S(2)}) collective-permute-start(bf16[1,2,2,1,512]{4,2,1,3,0:T(2,128)(2,1)S(1)} %maximum_bitcast_fusion.1), channel_id=1, source_target_pairs={{0,416},{32,384},{64,480},{96,448},{128,288},{160,256},{192,352},{... | collective-permute-start | bytes 12296 | tf_op jit(solution)/shard_map/ppermute | solution.py:20
  212.9 4.4 %collective-permute-start.28 = (bf16[1,2,2,1,512]{4,2,1,3,0:T(2,128)(2,1)S(1)}, bf16[1,2,2,1,512]{4,2,1,3,0:T(2,128)(2,1)S(1)}, u32[]{:S(2)}, u32[]{:S(2)}) collective-permute-start(bf16[1,2,2,1,512]{4,2,1,3,0:T(2,128)(2,1)S(1)} %maximum_bitcast_fusion.1), channel_id=1, source_target_pairs={{0,448},{32,480},{64,384},{96,416},{128,320},{160,352},{192,256},{... | collective-permute-start | bytes 12296 | tf_op jit(solution)/shard_map/ppermute | solution.py:20
  218.3 3.2 %collective-permute-start.29 = (bf16[1,2,2,1,512]{4,2,1,3,0:T(2,128)(2,1)S(1)}, bf16[1,2,2,1,512]{4,2,1,3,0:T(2,128)(2,1)S(1)}, u32[]{:S(2)}, u32[]{:S(2)}) collective-permute-start(bf16[1,2,2,1,512]{4,2,1,3,0:T(2,128)(2,1)S(1)} %maximum_bitcast_fusion.1), channel_id=1, source_target_pairs={{0,480},{32,448},{64,416},{96,384},{128,352},{160,320},{192,288},{... | collective-permute-start | bytes 12296 | tf_op jit(solution)/shard_map/ppermute | solution.py:20
  232.8 3.9 %convolution_bitcast_fusion = f32[2,1,512,512]{2,3,0,1:T(8,128)} fusion(bf16[1,2,512,512]{3,2,1,0:T(8,128)(2,1)S(1)} %copy-done, bf16[1,512,512]{1,2,0:T(8,128)(2,1)S(1)} %bitcast.107, bf16[1,512,512]{1,2,0:T(8,128)(2,1)S(1)} %bitcast.106, f32[2,512]{1,0:T(2,128)S(1)} %copy.185, f32[2,512]{1,0:T(2,128)S(1)} %copy.184, f32[2,512]{1,0:T(2,128)} %copy-done.4, ...), kind=kOutput, calls=%fused_computation.6 | convolution fusion | flops 1076887552 | bytes 5259264 | tf_op jit(solution)/shard_map/fcy,fzyx->fzcx/dot_general | solution.py:56
  236.7 3.8 %subtract_convert_fusion.1 = (bf16[1,1,512,512]{2,3,0,1:T(8,128)(2,1)S(1)}, bf16[1,1,512,512]{2,3,0,1:T(8,128)(2,1)S(1)}) fusion(f32[2,1,512,512]{2,3,0,1:T(8,128)} %convolution_bitcast_fusion, f32[]{:T(128)} %bitcast.27, f32[]{:T(128)} %bitcast.26, f32[]{:T(128)} %bitcast.30), kind=kLoop, calls=%fused_computation.16 | loop fusion | flops 2621440 | bytes 3145740 | tf_op jit(solution)/shard_map/convert.6
  241.6 28.6 %all_to_all.21 = bf16[2,1,512,512]{3,0,1,2:T(2,128)(2,1)S(1)} all-to-all(bf16[2,1,512,512]{3,0,1,2:T(2,128)(2,1)S(1)} %copy.187), channel_id=1, replica_groups=mesh['blk'=16,'pen'=32] {'pen'}, dimensions={2} | all-to-all | bytes 2097152 | tf_op jit(solution)/shard_map/all_to_all | solution.py:62
  (154 shorter events, 62.3 us)
Async XLA Ops:
  0.0 128.5 %copy-start = (bf16[1,2,512,512]{3,2,1,0:T(8,128)(2,1)S(1)}, bf16[1,2,512,512]{3,2,1,0:T(8,128)(2,1)}, u32[]{:S(2)}) copy-start(bf16[1,2,512,512]{3,2,1,0:T(8,128)(2,1)} %param.12) | copy-start | bytes 3145732
  2.5 27.5 %all-to-all-start = ((bf16[2,32,16,512]{3,2,0,1:T(8,128)(2,1)}), bf16[2,32,16,512]{3,2,0,1:T(8,128)(2,1)S(1)}, u32[]{:S(2)}, u32[]{:S(2)}) async-start(bf16[2,32,16,512]{3,2,0,1:T(8,128)(2,1)} %bitcast.101), calls=%async_computation | async-start | bytes 2097152 | tf_op jit(solution)/shard_map/all_to_all | solution.py:48
  30.6 22.8 %collective-permute-start = (bf16[1,2,2,1,512]{4,2,1,3,0:T(2,128)(2,1)S(1)}, bf16[1,2,2,1,512]{4,2,1,3,0:T(2,128)(2,1)S(1)}, u32[]{:S(2)}, u32[]{:S(2)}) collective-permute-start(bf16[1,2,2,1,512]{4,2,1,3,0:T(2,128)(2,1)S(1)} %maximum_bitcast_fusion), channel_id=1, source_target_pairs={{0,32},{32,0},{64,96},{96,64},{128,160},{160,128},{192,224},{224,1... | collective-permute-start | bytes 12296 | tf_op jit(solution)/shard_map/ppermute | solution.py:20
  32.5 31.2 %collective-permute-start.1 = (bf16[1,2,2,1,512]{4,2,1,3,0:T(2,128)(2,1)S(1)}, bf16[1,2,2,1,512]{4,2,1,3,0:T(2,128)(2,1)S(1)}, u32[]{:S(2)}, u32[]{:S(2)}) collective-permute-start(bf16[1,2,2,1,512]{4,2,1,3,0:T(2,128)(2,1)S(1)} %maximum_bitcast_fusion), channel_id=1, source_target_pairs={{0,64},{32,96},{64,0},{96,32},{128,192},{160,224},{192,128},{224,1... | collective-permute-start | bytes 12296 | tf_op jit(solution)/shard_map/ppermute | solution.py:20
  37.1 29.5 %collective-permute-start.2 = (bf16[1,2,2,1,512]{4,2,1,3,0:T(2,128)(2,1)S(1)}, bf16[1,2,2,1,512]{4,2,1,3,0:T(2,128)(2,1)S(1)}, u32[]{:S(2)}, u32[]{:S(2)}) collective-permute-start(bf16[1,2,2,1,512]{4,2,1,3,0:T(2,128)(2,1)S(1)} %maximum_bitcast_fusion), channel_id=1, source_target_pairs={{0,96},{32,64},{64,32},{96,0},{128,224},{160,192},{192,160},{224,1... | collective-permute-start | bytes 12296 | tf_op jit(solution)/shard_map/ppermute | solution.py:20
  39.9 40.2 %collective-permute-start.3 = (bf16[1,2,2,1,512]{4,2,1,3,0:T(2,128)(2,1)S(1)}, bf16[1,2,2,1,512]{4,2,1,3,0:T(2,128)(2,1)S(1)}, u32[]{:S(2)}, u32[]{:S(2)}) collective-permute-start(bf16[1,2,2,1,512]{4,2,1,3,0:T(2,128)(2,1)S(1)} %maximum_bitcast_fusion), channel_id=1, source_target_pairs={{0,128},{32,160},{64,192},{96,224},{128,0},{160,32},{192,64},{224,... | collective-permute-start | bytes 12296 | tf_op jit(solution)/shard_map/ppermute | solution.py:20
  47.8 35.1 %collective-permute-start.4 = (bf16[1,2,2,1,512]{4,2,1,3,0:T(2,128)(2,1)S(1)}, bf16[1,2,2,1,512]{4,2,1,3,0:T(2,128)(2,1)S(1)}, u32[]{:S(2)}, u32[]{:S(2)}) collective-permute-start(bf16[1,2,2,1,512]{4,2,1,3,0:T(2,128)(2,1)S(1)} %maximum_bitcast_fusion), channel_id=1, source_target_pairs={{0,160},{32,128},{64,224},{96,192},{128,32},{160,0},{192,96},{224,... | collective-permute-start | bytes 12296 | tf_op jit(solution)/shard_map/ppermute | solution.py:20
  53.4 37.6 %collective-permute-start.5 = (bf16[1,2,2,1,512]{4,2,1,3,0:T(2,128)(2,1)S(1)}, bf16[1,2,2,1,512]{4,2,1,3,0:T(2,128)(2,1)S(1)}, u32[]{:S(2)}, u32[]{:S(2)}) collective-permute-start(bf16[1,2,2,1,512]{4,2,1,3,0:T(2,128)(2,1)S(1)} %maximum_bitcast_fusion), channel_id=1, source_target_pairs={{0,192},{32,224},{64,128},{96,160},{128,64},{160,96},{192,0},{224,... | collective-permute-start | bytes 12296 | tf_op jit(solution)/shard_map/ppermute | solution.py:20
  63.7 32.4 %collective-permute-start.6 = (bf16[1,2,2,1,512]{4,2,1,3,0:T(2,128)(2,1)S(1)}, bf16[1,2,2,1,512]{4,2,1,3,0:T(2,128)(2,1)S(1)}, u32[]{:S(2)}, u32[]{:S(2)}) collective-permute-start(bf16[1,2,2,1,512]{4,2,1,3,0:T(2,128)(2,1)S(1)} %maximum_bitcast_fusion), channel_id=1, source_target_pairs={{0,224},{32,192},{64,160},{96,128},{128,96},{160,64},{192,32},{224... | collective-permute-start | bytes 12296 | tf_op jit(solution)/shard_map/ppermute | solution.py:20
  66.5 35.9 %collective-permute-start.7 = (bf16[1,2,2,1,512]{4,2,1,3,0:T(2,128)(2,1)S(1)}, bf16[1,2,2,1,512]{4,2,1,3,0:T(2,128)(2,1)S(1)}, u32[]{:S(2)}, u32[]{:S(2)}) collective-permute-start(bf16[1,2,2,1,512]{4,2,1,3,0:T(2,128)(2,1)S(1)} %maximum_bitcast_fusion), channel_id=1, source_target_pairs={{0,256},{32,288},{64,320},{96,352},{128,384},{160,416},{192,448},{... | collective-permute-start | bytes 12296 | tf_op jit(solution)/shard_map/ppermute | solution.py:20
  80.0 28.0 %collective-permute-start.8 = (bf16[1,2,2,1,512]{4,2,1,3,0:T(2,128)(2,1)S(1)}, bf16[1,2,2,1,512]{4,2,1,3,0:T(2,128)(2,1)S(1)}, u32[]{:S(2)}, u32[]{:S(2)}) collective-permute-start(bf16[1,2,2,1,512]{4,2,1,3,0:T(2,128)(2,1)S(1)} %maximum_bitcast_fusion), channel_id=1, source_target_pairs={{0,288},{32,256},{64,352},{96,320},{128,416},{160,384},{192,480},{... | collective-permute-start | bytes 12296 | tf_op jit(solution)/shard_map/ppermute | solution.py:20
  82.9 33.9 %collective-permute-start.9 = (bf16[1,2,2,1,512]{4,2,1,3,0:T(2,128)(2,1)S(1)}, bf16[1,2,2,1,512]{4,2,1,3,0:T(2,128)(2,1)S(1)}, u32[]{:S(2)}, u32[]{:S(2)}) collective-permute-start(bf16[1,2,2,1,512]{4,2,1,3,0:T(2,128)(2,1)S(1)} %maximum_bitcast_fusion), channel_id=1, source_target_pairs={{0,320},{32,352},{64,256},{96,288},{128,448},{160,480},{192,384},{... | collective-permute-start | bytes 12296 | tf_op jit(solution)/shard_map/ppermute | solution.py:20
  91.0 28.6 %collective-permute-start.10 = (bf16[1,2,2,1,512]{4,2,1,3,0:T(2,128)(2,1)S(1)}, bf16[1,2,2,1,512]{4,2,1,3,0:T(2,128)(2,1)S(1)}, u32[]{:S(2)}, u32[]{:S(2)}) collective-permute-start(bf16[1,2,2,1,512]{4,2,1,3,0:T(2,128)(2,1)S(1)} %maximum_bitcast_fusion), channel_id=1, source_target_pairs={{0,352},{32,320},{64,288},{96,256},{128,480},{160,448},{192,416},{... | collective-permute-start | bytes 12296 | tf_op jit(solution)/shard_map/ppermute | solution.py:20
  96.1 24.5 %collective-permute-start.11 = (bf16[1,2,2,1,512]{4,2,1,3,0:T(2,128)(2,1)S(1)}, bf16[1,2,2,1,512]{4,2,1,3,0:T(2,128)(2,1)S(1)}, u32[]{:S(2)}, u32[]{:S(2)}) collective-permute-start(bf16[1,2,2,1,512]{4,2,1,3,0:T(2,128)(2,1)S(1)} %maximum_bitcast_fusion), channel_id=1, source_target_pairs={{0,384},{32,416},{64,448},{96,480},{128,256},{160,288},{192,320},{... | collective-permute-start | bytes 12296 | tf_op jit(solution)/shard_map/ppermute | solution.py:20
  102.5 19.0 %collective-permute-start.12 = (bf16[1,2,2,1,512]{4,2,1,3,0:T(2,128)(2,1)S(1)}, bf16[1,2,2,1,512]{4,2,1,3,0:T(2,128)(2,1)S(1)}, u32[]{:S(2)}, u32[]{:S(2)}) collective-permute-start(bf16[1,2,2,1,512]{4,2,1,3,0:T(2,128)(2,1)S(1)} %maximum_bitcast_fusion), channel_id=1, source_target_pairs={{0,416},{32,384},{64,480},{96,448},{128,288},{160,256},{192,352},{... | collective-permute-start | bytes 12296 | tf_op jit(solution)/shard_map/ppermute | solution.py:20
  108.0 14.4 %collective-permute-start.13 = (bf16[1,2,2,1,512]{4,2,1,3,0:T(2,128)(2,1)S(1)}, bf16[1,2,2,1,512]{4,2,1,3,0:T(2,128)(2,1)S(1)}, u32[]{:S(2)}, u32[]{:S(2)}) collective-permute-start(bf16[1,2,2,1,512]{4,2,1,3,0:T(2,128)(2,1)S(1)} %maximum_bitcast_fusion), channel_id=1, source_target_pairs={{0,448},{32,480},{64,384},{96,416},{128,320},{160,352},{192,256},{... | collective-permute-start | bytes 12296 | tf_op jit(solution)/shard_map/ppermute | solution.py:20
  116.7 6.6 %collective-permute-start.14 = (bf16[1,2,2,1,512]{4,2,1,3,0:T(2,128)(2,1)S(1)}, bf16[1,2,2,1,512]{4,2,1,3,0:T(2,128)(2,1)S(1)}, u32[]{:S(2)}, u32[]{:S(2)}) collective-permute-start(bf16[1,2,2,1,512]{4,2,1,3,0:T(2,128)(2,1)S(1)} %maximum_bitcast_fusion), channel_id=1, source_target_pairs={{0,480},{32,448},{64,416},{96,384},{128,352},{160,320},{192,288},{... | collective-permute-start | bytes 12296 | tf_op jit(solution)/shard_map/ppermute | solution.py:20
  136.6 23.3 %collective-permute-start.15 = (bf16[1,2,2,1,512]{4,2,1,3,0:T(2,128)(2,1)S(1)}, bf16[1,2,2,1,512]{4,2,1,3,0:T(2,128)(2,1)S(1)}, u32[]{:S(2)}, u32[]{:S(2)}) collective-permute-start(bf16[1,2,2,1,512]{4,2,1,3,0:T(2,128)(2,1)S(1)} %maximum_bitcast_fusion.1), channel_id=1, source_target_pairs={{0,32},{32,0},{64,96},{96,64},{128,160},{160,128},{192,224},{224,1... | collective-permute-start | bytes 12296 | tf_op jit(solution)/shard_map/ppermute | solution.py:20
  139.6 26.7 %collective-permute-start.16 = (bf16[1,2,2,1,512]{4,2,1,3,0:T(2,128)(2,1)S(1)}, bf16[1,2,2,1,512]{4,2,1,3,0:T(2,128)(2,1)S(1)}, u32[]{:S(2)}, u32[]{:S(2)}) collective-permute-start(bf16[1,2,2,1,512]{4,2,1,3,0:T(2,128)(2,1)S(1)} %maximum_bitcast_fusion.1), channel_id=1, source_target_pairs={{0,64},{32,96},{64,0},{96,32},{128,192},{160,224},{192,128},{224,1... | collective-permute-start | bytes 12296 | tf_op jit(solution)/shard_map/ppermute | solution.py:20
  145.1 27.6 %collective-permute-start.17 = (bf16[1,2,2,1,512]{4,2,1,3,0:T(2,128)(2,1)S(1)}, bf16[1,2,2,1,512]{4,2,1,3,0:T(2,128)(2,1)S(1)}, u32[]{:S(2)}, u32[]{:S(2)}) collective-permute-start(bf16[1,2,2,1,512]{4,2,1,3,0:T(2,128)(2,1)S(1)} %maximum_bitcast_fusion.1), channel_id=1, source_target_pairs={{0,96},{32,64},{64,32},{96,0},{128,224},{160,192},{192,160},{224,1... | collective-permute-start | bytes 12296 | tf_op jit(solution)/shard_map/ppermute | solution.py:20
  147.0 34.5 %collective-permute-start.18 = (bf16[1,2,2,1,512]{4,2,1,3,0:T(2,128)(2,1)S(1)}, bf16[1,2,2,1,512]{4,2,1,3,0:T(2,128)(2,1)S(1)}, u32[]{:S(2)}, u32[]{:S(2)}) collective-permute-start(bf16[1,2,2,1,512]{4,2,1,3,0:T(2,128)(2,1)S(1)} %maximum_bitcast_fusion.1), channel_id=1, source_target_pairs={{0,128},{32,160},{64,192},{96,224},{128,0},{160,32},{192,64},{224,... | collective-permute-start | bytes 12296 | tf_op jit(solution)/shard_map/ppermute | solution.py:20
  153.8 33.9 %collective-permute-start.19 = (bf16[1,2,2,1,512]{4,2,1,3,0:T(2,128)(2,1)S(1)}, bf16[1,2,2,1,512]{4,2,1,3,0:T(2,128)(2,1)S(1)}, u32[]{:S(2)}, u32[]{:S(2)}) collective-permute-start(bf16[1,2,2,1,512]{4,2,1,3,0:T(2,128)(2,1)S(1)} %maximum_bitcast_fusion.1), channel_id=1, source_target_pairs={{0,160},{32,128},{64,224},{96,192},{128,32},{160,0},{192,96},{224,... | collective-permute-start | bytes 12296 | tf_op jit(solution)/shard_map/ppermute | solution.py:20
  159.8 34.2 %collective-permute-start.20 = (bf16[1,2,2,1,512]{4,2,1,3,0:T(2,128)(2,1)S(1)}, bf16[1,2,2,1,512]{4,2,1,3,0:T(2,128)(2,1)S(1)}, u32[]{:S(2)}, u32[]{:S(2)}) collective-permute-start(bf16[1,2,2,1,512]{4,2,1,3,0:T(2,128)(2,1)S(1)} %maximum_bitcast_fusion.1), channel_id=1, source_target_pairs={{0,192},{32,224},{64,128},{96,160},{128,64},{160,96},{192,0},{224,... | collective-permute-start | bytes 12296 | tf_op jit(solution)/shard_map/ppermute | solution.py:20
  166.4 35.4 %collective-permute-start.21 = (bf16[1,2,2,1,512]{4,2,1,3,0:T(2,128)(2,1)S(1)}, bf16[1,2,2,1,512]{4,2,1,3,0:T(2,128)(2,1)S(1)}, u32[]{:S(2)}, u32[]{:S(2)}) collective-permute-start(bf16[1,2,2,1,512]{4,2,1,3,0:T(2,128)(2,1)S(1)} %maximum_bitcast_fusion.1), channel_id=1, source_target_pairs={{0,224},{32,192},{64,160},{96,128},{128,96},{160,64},{192,32},{224... | collective-permute-start | bytes 12296 | tf_op jit(solution)/shard_map/ppermute | solution.py:20
  172.7 32.9 %collective-permute-start.22 = (bf16[1,2,2,1,512]{4,2,1,3,0:T(2,128)(2,1)S(1)}, bf16[1,2,2,1,512]{4,2,1,3,0:T(2,128)(2,1)S(1)}, u32[]{:S(2)}, u32[]{:S(2)}) collective-permute-start(bf16[1,2,2,1,512]{4,2,1,3,0:T(2,128)(2,1)S(1)} %maximum_bitcast_fusion.1), channel_id=1, source_target_pairs={{0,256},{32,288},{64,320},{96,352},{128,384},{160,416},{192,448},{... | collective-permute-start | bytes 12296 | tf_op jit(solution)/shard_map/ppermute | solution.py:20
  181.4 31.5 %collective-permute-start.23 = (bf16[1,2,2,1,512]{4,2,1,3,0:T(2,128)(2,1)S(1)}, bf16[1,2,2,1,512]{4,2,1,3,0:T(2,128)(2,1)S(1)}, u32[]{:S(2)}, u32[]{:S(2)}) collective-permute-start(bf16[1,2,2,1,512]{4,2,1,3,0:T(2,128)(2,1)S(1)} %maximum_bitcast_fusion.1), channel_id=1, source_target_pairs={{0,288},{32,256},{64,352},{96,320},{128,416},{160,384},{192,480},{... | collective-permute-start | bytes 12296 | tf_op jit(solution)/shard_map/ppermute | solution.py:20
  187.7 30.7 %collective-permute-start.24 = (bf16[1,2,2,1,512]{4,2,1,3,0:T(2,128)(2,1)S(1)}, bf16[1,2,2,1,512]{4,2,1,3,0:T(2,128)(2,1)S(1)}, u32[]{:S(2)}, u32[]{:S(2)}) collective-permute-start(bf16[1,2,2,1,512]{4,2,1,3,0:T(2,128)(2,1)S(1)} %maximum_bitcast_fusion.1), channel_id=1, source_target_pairs={{0,320},{32,352},{64,256},{96,288},{128,448},{160,480},{192,384},{... | collective-permute-start | bytes 12296 | tf_op jit(solution)/shard_map/ppermute | solution.py:20
  194.0 28.5 %collective-permute-start.25 = (bf16[1,2,2,1,512]{4,2,1,3,0:T(2,128)(2,1)S(1)}, bf16[1,2,2,1,512]{4,2,1,3,0:T(2,128)(2,1)S(1)}, u32[]{:S(2)}, u32[]{:S(2)}) collective-permute-start(bf16[1,2,2,1,512]{4,2,1,3,0:T(2,128)(2,1)S(1)} %maximum_bitcast_fusion.1), channel_id=1, source_target_pairs={{0,352},{32,320},{64,288},{96,256},{128,480},{160,448},{192,416},{... | collective-permute-start | bytes 12296 | tf_op jit(solution)/shard_map/ppermute | solution.py:20
  201.8 21.6 %collective-permute-start.26 = (bf16[1,2,2,1,512]{4,2,1,3,0:T(2,128)(2,1)S(1)}, bf16[1,2,2,1,512]{4,2,1,3,0:T(2,128)(2,1)S(1)}, u32[]{:S(2)}, u32[]{:S(2)}) collective-permute-start(bf16[1,2,2,1,512]{4,2,1,3,0:T(2,128)(2,1)S(1)} %maximum_bitcast_fusion.1), channel_id=1, source_target_pairs={{0,384},{32,416},{64,448},{96,480},{128,256},{160,288},{192,320},{... | collective-permute-start | bytes 12296 | tf_op jit(solution)/shard_map/ppermute | solution.py:20
  205.6 18.8 %collective-permute-start.27 = (bf16[1,2,2,1,512]{4,2,1,3,0:T(2,128)(2,1)S(1)}, bf16[1,2,2,1,512]{4,2,1,3,0:T(2,128)(2,1)S(1)}, u32[]{:S(2)}, u32[]{:S(2)}) collective-permute-start(bf16[1,2,2,1,512]{4,2,1,3,0:T(2,128)(2,1)S(1)} %maximum_bitcast_fusion.1), channel_id=1, source_target_pairs={{0,416},{32,384},{64,480},{96,448},{128,288},{160,256},{192,352},{... | collective-permute-start | bytes 12296 | tf_op jit(solution)/shard_map/ppermute | solution.py:20
  212.9 12.4 %collective-permute-start.28 = (bf16[1,2,2,1,512]{4,2,1,3,0:T(2,128)(2,1)S(1)}, bf16[1,2,2,1,512]{4,2,1,3,0:T(2,128)(2,1)S(1)}, u32[]{:S(2)}, u32[]{:S(2)}) collective-permute-start(bf16[1,2,2,1,512]{4,2,1,3,0:T(2,128)(2,1)S(1)} %maximum_bitcast_fusion.1), channel_id=1, source_target_pairs={{0,448},{32,480},{64,384},{96,416},{128,320},{160,352},{192,256},{... | collective-permute-start | bytes 12296 | tf_op jit(solution)/shard_map/ppermute | solution.py:20
  218.3 7.9 %collective-permute-start.29 = (bf16[1,2,2,1,512]{4,2,1,3,0:T(2,128)(2,1)S(1)}, bf16[1,2,2,1,512]{4,2,1,3,0:T(2,128)(2,1)S(1)}, u32[]{:S(2)}, u32[]{:S(2)}) collective-permute-start(bf16[1,2,2,1,512]{4,2,1,3,0:T(2,128)(2,1)S(1)} %maximum_bitcast_fusion.1), channel_id=1, source_target_pairs={{0,480},{32,448},{64,416},{96,384},{128,352},{160,320},{192,288},{... | collective-permute-start | bytes 12296 | tf_op jit(solution)/shard_map/ppermute | solution.py:20
  (8 other events, 254.1 us)
